TPU v7x, 512 devices: a whole 4x8x8 slice. The times are simulated.
512 devices in a mesh: section: 2 (over y_lo), sample: 16 (over z, core), seq: 16 (over x, y_hi).
Axes of the slice: x: 4, y: 8 (y_hi: 4, y_lo: 2; y = y_hi * 2 + y_lo), z: 8, core: 2. Of those that a mesh axis runs over, the one named last changes fastest.
Arguments:
- first_rows: bfloat16 [2, 16, 2048, 2048], P('section', 'sample', 'seq'), may hold values from -10 to 10
- second_rows: bfloat16 [2, 16, 2048, 2048], P('section', 'sample', 'seq'), may hold values from -6 to 6
- alignment: int32 [16, 16, 2], P('sample', 'seq'), may hold values from 0 to 15, as said below
- diffusion_mask: int32 [16, 2048], P('sample', 'seq'), may hold values 0 or 1
- source_length: int32 [16], P('sample'), may hold values from 1024 to 2048, as said below
- target_length: int32 [16], P('sample'), may hold values from 1024 to 2048
Outputs:
- grad_first: bfloat16 [2, 16, 2048, 2048], P('section', 'sample', 'seq')
- grad_second: bfloat16 [2, 16, 2048, 2048], P('section', 'sample', 'seq')
Inputs may be any that keep to these rules, and one draw needn't show every extreme that they name: `alignment`: each list names 2 different blocks from t - 1 to t + 1 for target block t; where block t holds a target position below the target length, every listed block starts below the source length. `source_length`: at least the sample's target length.
All inputs are finite; a program needn't handle non-finite values. No bound on the sum of `diffusion_mask` on one device may be relied on, other than what follows from the above.
Results may differ from a plain program's by a relative error of at most 0.013.
Values may be sent and summed in bfloat16 or wider, within the bound.
A program may use at most 64 MiB of HBM per device.

v0:
```python
import jax
import jax.numpy as jnp
from jax import lax
from jax.sharding import PartitionSpec as P

HEADS = 32
HDIM = 64
INNER = 2048
BLK = 128
NLIST = 2
WIN = 1


def shifted(array, axis, by):
    count = lax.axis_size(axis)
    pairs = [(i, i + by) for i in range(count) if 0 <= i + by < count]
    return lax.ppermute(array, axis, pairs)


def padded(array, sides, width):
    for axis, dim in sides:
        count, length = (lax.axis_size(axis), array.shape[dim])
        up = [(i, (i + 1) % count) for i in range(count - 1)]
        down = [(j, i) for i, j in up]
        last = lax.slice_in_dim(array, length - width, length, axis=dim)
        first = lax.slice_in_dim(array, 0, width, axis=dim)
        before = lax.ppermute(last, axis, up)
        after = lax.ppermute(first, axis, down)
        array = jnp.concatenate([before, array, after], axis=dim)
    return array


def attend_local(query_blk, cot_blk, key_rows, value_rows, key_valid, query_valid, cot_keep):
    scale = HDIM ** (-0.5)
    queries = query_blk.reshape(BLK, HEADS, HDIM)
    keys = key_rows.reshape(NLIST * BLK, HEADS, HDIM)
    values = value_rows.reshape(NLIST * BLK, HEADS, HDIM)
    scores = jnp.einsum("qhd,khd->hqk", queries, keys, preferred_element_type=jnp.float32) * scale
    scores = jnp.where(key_valid[None, None, :], scores, -1e30)
    peak = jnp.max(scores, axis=-1, keepdims=True)
    expo = jnp.exp(scores - peak)
    probs = expo / jnp.sum(expo, axis=-1, keepdims=True)
    probs_low = probs.astype(jnp.bfloat16)
    attended = jnp.einsum("hqk,khd->qhd", probs_low, values, preferred_element_type=jnp.float32)
    attended = jnp.where(query_valid[:, None, None], attended, jnp.float32(0.0))
    out_low = attended.astype(jnp.bfloat16)
    cot = cot_blk.reshape(BLK, HEADS, HDIM)
    cot = jnp.where(cot_keep[:, None, None], cot, jnp.zeros_like(cot))
    delta = jnp.einsum("qhd,qhd->hq", cot, out_low, preferred_element_type=jnp.float32)[:, :, None]
    dprob = jnp.einsum("qhd,khd->hqk", cot, values, preferred_element_type=jnp.float32)
    dscore_low = (probs * (dprob - delta)).astype(jnp.bfloat16)
    dvalue = jnp.einsum("hqk,qhd->khd", probs_low, cot, preferred_element_type=jnp.float32)
    dquery = (
        jnp.einsum("hqk,khd->qhd", dscore_low, keys, preferred_element_type=jnp.float32) * scale
    )
    dkey = (
        jnp.einsum("hqk,qhd->khd", dscore_low, queries, preferred_element_type=jnp.float32) * scale
    )
    return (
        out_low.reshape(BLK, INNER),
        dquery.astype(jnp.bfloat16).reshape(BLK, INNER),
        dkey.reshape(NLIST * BLK, INNER),
        dvalue.reshape(NLIST * BLK, INNER),
    )


def on_device(first_rows, second_rows, alignment, diffusion_mask, source_length, target_length):
    rows_here = first_rows.shape[2]
    width = first_rows.shape[3]
    block_count = alignment.shape[1]
    rim = WIN * BLK
    section_id = lax.axis_index("section")
    shard_id = lax.axis_index("seq")
    on_encoder = section_id == 0
    holding = jnp.stack([first_rows[0, 0], second_rows[0, 0]])
    memory = shifted(holding, "section", 1)
    window = padded(memory, (("seq", 1),), rim)
    window_start = shard_id * rows_here - rim
    source_len = source_length[0]
    target_len = target_length[0]
    query_blocks = holding[0].reshape(block_count, BLK, width)
    cot_blocks = holding[1].reshape(block_count, BLK, width)
    mask_blocks = diffusion_mask[0].reshape(block_count, BLK)
    lists_here = alignment[0]
    inside = jnp.arange(BLK, dtype=jnp.int32)

    def step(carry, index):
        key_grad, value_grad = carry
        chosen = lists_here[index]
        starts = [chosen[slot] * BLK - window_start for slot in range(NLIST)]
        key_rows = jnp.concatenate(
            [lax.dynamic_slice_in_dim(window[0], starts[slot], BLK, 0) for slot in range(NLIST)], 0
        )
        value_rows = jnp.concatenate(
            [lax.dynamic_slice_in_dim(window[1], starts[slot], BLK, 0) for slot in range(NLIST)], 0
        )
        key_pos = (chosen[:, None] * BLK + inside[None, :]).reshape(NLIST * BLK)
        key_valid = key_pos < source_len
        row_pos = (shard_id * block_count + index) * BLK + inside
        query_valid = row_pos < target_len
        cot_keep = query_valid & (mask_blocks[index] == 1)
        out_low, dquery, dkey, dvalue = attend_local(
            query_blocks[index],
            cot_blocks[index],
            key_rows,
            value_rows,
            key_valid,
            query_valid,
            cot_keep,
        )
        for slot in range(NLIST):
            older_key = lax.dynamic_slice_in_dim(key_grad, starts[slot], BLK, 0)
            key_grad = lax.dynamic_update_slice_in_dim(
                key_grad, older_key + dkey[slot * BLK : (slot + 1) * BLK], starts[slot], 0
            )
            older_value = lax.dynamic_slice_in_dim(value_grad, starts[slot], BLK, 0)
            value_grad = lax.dynamic_update_slice_in_dim(
                value_grad, older_value + dvalue[slot * BLK : (slot + 1) * BLK], starts[slot], 0
            )
        return ((key_grad, value_grad), (out_low, dquery))

    span = rows_here + 2 * rim
    start = (jnp.zeros((span, width), jnp.float32), jnp.zeros((span, width), jnp.float32))
    (key_grad, value_grad), (outs, dqueries) = lax.scan(
        step, start, jnp.arange(block_count, dtype=jnp.int32)
    )
    grads = jnp.stack([key_grad, value_grad])
    middle = grads[:, rim : rim + rows_here]
    from_below = shifted(grads[:, rows_here + rim :], "seq", 1)
    from_above = shifted(grads[:, :rim], "seq", -1)
    middle = middle.at[:, :rim].add(from_below)
    middle = middle.at[:, rows_here - rim :].add(from_above)
    memory_grads = middle.astype(jnp.bfloat16)
    memory_grads = shifted(memory_grads, "section", -1)
    first_out = jnp.where(on_encoder, memory_grads[0], dqueries.reshape(rows_here, width))
    second_out = jnp.where(on_encoder, memory_grads[1], outs.reshape(rows_here, width))
    return (first_out[None, None], second_out[None, None])


def solution(mesh):
    placed = (
        P("section", "sample", "seq", None),
        P("section", "sample", "seq", None),
        P("sample", "seq", None),
        P("sample", "seq"),
        P("sample"),
        P("sample"),
    )
    return jax.shard_map(
        on_device,
        mesh=mesh,
        in_specs=placed,
        out_specs=(P("section", "sample", "seq", None), P("section", "sample", "seq", None)),
        check_vma=False,
    )
```

profile of v0, /device:TPU:450, one launch (start us, length us, event | category | flops | bytes accessed | tf_op | source)
XLA Modules:
  0.0 247.9 jit_solution(17976209204909602213)
XLA Ops:
  0.6 0.0 copy-start.5
  0.6 0.0 copy-start.7
  0.7 1.4 pad_maximum_fusion.1
  2.0 3.5 %collective-permute-start = (bf16[2,128,2048]{2,1,0:T(8,128)(2,1)S(1)}, bf16[2,128,2048]{2,1,0:T(8,128)(2,1)S(1)}, u32[]{:S(2)}, u32[]{:S(2)}) collective-permute-start(bf16[2,128,2048]{2,1,0:T(8,128)(2,1)S(1)} %pad_maximum_fusion.1), channel_id=1, source_target_pairs={{0,256},{1,257},{2,258},{3,259},{4,260},{5,261},{6,262},{7,263},{8... | collective-permute-start | bytes 3145736 | tf_op jit(solution)/shard_map/ppermute | solution.py:17
  5.6 22.3 %collective-permute-done = bf16[2,128,2048]{2,1,0:T(8,128)(2,1)S(1)} collective-permute-done((bf16[2,128,2048]{2,1,0:T(8,128)(2,1)S(1)}, bf16[2,128,2048]{2,1,0:T(8,128)(2,1)S(1)}, u32[]{:S(2)}, u32[]{:S(2)}) %collective-permute-start) | collective-permute-done | bytes 1048608 | tf_op jit(solution)/shard_map/ppermute | solution.py:17
  27.9 4.5 %collective-permute-start.1 = (bf16[2,128,2048]{2,1,0:T(8,128)(2,1)S(1)}, bf16[2,128,2048]{2,1,0:T(8,128)(2,1)}, u32[]{:S(2)}, u32[]{:S(2)}) collective-permute-start(bf16[2,128,2048]{2,1,0:T(8,128)(2,1)S(1)} %collective-permute-done), channel_id=1, source_target_pairs={{0,1},{1,2},{2,3},{3,4},{4,5},{5,6},{6,7},{7,8},{8,9},{9,10},{10,1... | collective-permute-start | bytes 3145736 | tf_op jit(solution)/shard_map/ppermute | solution.py:27
  32.4 1.3 copy.29
  33.7 0.0 copy-done.5
  33.7 0.3 copy.28
  34.0 4.4 %collective-permute-start.2 = (bf16[2,128,2048]{2,1,0:T(8,128)(2,1)S(1)}, bf16[2,128,2048]{2,1,0:T(8,128)(2,1)}, u32[]{:S(2)}, u32[]{:S(2)}) collective-permute-start(bf16[2,128,2048]{2,1,0:T(8,128)(2,1)S(1)} %collective-permute-done), channel_id=1, source_target_pairs={{1,0},{2,1},{3,2},{4,3},{5,4},{6,5},{7,6},{8,7},{9,8},{10,9},{11,1... | collective-permute-start | bytes 3145736 | tf_op jit(solution)/shard_map/ppermute | solution.py:28
  38.4 0.6 fusion.33
  41.6 0.1 compare_bitcast_fusion
  41.7 0.0 copy-done.8
  41.7 15.5 %collective-permute-done.1 = bf16[2,128,2048]{2,1,0:T(8,128)(2,1)} collective-permute-done((bf16[2,128,2048]{2,1,0:T(8,128)(2,1)S(1)}, bf16[2,128,2048]{2,1,0:T(8,128)(2,1)}, u32[]{:S(2)}, u32[]{:S(2)}) %collective-permute-start.1) | collective-permute-done | bytes 1048608 | tf_op jit(solution)/shard_map/ppermute | solution.py:27
  57.2 1.3 constant_dynamic-update-slice_fusion.2
  58.5 0.1 constant_dynamic-update-slice_fusion.1
  58.6 11.4 %collective-permute-done.2 = bf16[2,128,2048]{2,1,0:T(8,128)(2,1)} collective-permute-done((bf16[2,128,2048]{2,1,0:T(8,128)(2,1)S(1)}, bf16[2,128,2048]{2,1,0:T(8,128)(2,1)}, u32[]{:S(2)}, u32[]{:S(2)}) %collective-permute-start.2) | collective-permute-done | bytes 1048608 | tf_op jit(solution)/shard_map/ppermute | solution.py:28
  70.0 1.3 constant_dynamic-update-slice_fusion
  71.4 0.4 fusion.30
  71.8 0.1 constant_dynamic-slice_fusion.1
  71.9 1.0 copy.27
  72.9 1.0 copy.26
  73.9 0.3 copy.31
  74.2 0.3 copy.30
  74.5 0.0 copy-done.6
  74.5 1.8 fusion.17
  76.3 1.7 fusion.34
  78.0 0.5 fusion.13
  78.5 2.2 convolution_bitcast_fusion
  80.7 1.3 fusion.16
  82.1 1.0 multiply_convert_fusion
  83.1 0.0 copy-start.4
  83.1 0.8 multiply_bitcast_fusion
  84.0 1.3 fusion.31
  85.3 0.3 copy.35
  85.6 0.4 broadcast.163.clone
  86.0 0.1 constant_dynamic-update-slice_fusion.4
  86.1 0.2 copy.58
  86.3 1.4 copy-done.2
  87.7 2.6 %copy.36 = f32[128,2048]{1,0:T(8,128)} copy(f32[128,2048]{0,1:T(8,128)} %bitcast.75) | data formatting | bytes 2097152 | tf_op jit(solution)/shard_map/while/body/eval_jaxpr/slice | solution.py:114
  90.3 3.2 %fusion.32 = (f32[128,32,64]{0,2,1:T(8,128)}, f32[128,32,64]{0,2,1:T(8,128)}) fusion(f32[256,32,64]{0,2,1:T(8,128)} %convolution_bitcast_fusion), kind=kLoop, calls=%fused_computation.66 | loop fusion | bytes 4194304 | tf_op jit(solution)/shard_map/while/body/eval_jaxpr/slice | solution.py:118
  93.5 2.6 %copy.38 = f32[128,2048]{1,0:T(8,128)} copy(f32[128,2048]{0,1:T(8,128)} %bitcast.77) | data formatting | bytes 2097152 | tf_op jit(solution)/shard_map/while/body/eval_jaxpr/slice | solution.py:118
  96.1 0.4 broadcast.163.clone.1
  96.4 0.9 copy-done.3
  97.3 0.1 constant_dynamic-update-slice_fusion.3
  97.4 0.0 copy-start.1
  97.4 1.7 copy.60
  99.1 1.1 copy-done.1
  100.2 2.5 %copy.39 = f32[128,2048]{1,0:T(8,128)} copy(f32[128,2048]{0,1:T(8,128)} %bitcast.74) | data formatting | bytes 2097152 | tf_op jit(solution)/shard_map/while/body/eval_jaxpr/slice | solution.py:118
  102.7 1.8 bitcast_dynamic-update-slice_fusion.1
  104.5 0.7 copy-done
  105.2 1.7 bitcast_dynamic-update-slice_fusion
  106.9 0.5 fusion.5
  107.4 15.3 %collective-permute-start.4 = (f32[2,128,2048]{2,1,0:T(8,128)S(1)}, f32[2,128,2048]{2,1,0:T(8,128)S(1)}, u32[]{:S(2)}, u32[]{:S(2)}) collective-permute-start(f32[2,128,2048]{2,1,0:T(8,128)S(1)} %get-tuple-element.90), channel_id=1, source_target_pairs={{1,0},{2,1},{3,2},{4,3},{5,4},{6,5},{7,6},{8,7},{9,8},{10,9},{11,1... | collective-permute-start | bytes 6291464 | tf_op jit(solution)/shard_map/ppermute | solution.py:17
  122.7 6.0 %collective-permute-start.3 = (f32[2,128,2048]{2,1,0:T(8,128)S(1)}, f32[2,128,2048]{2,1,0:T(8,128)S(1)}, u32[]{:S(2)}, u32[]{:S(2)}) collective-permute-start(f32[2,128,2048]{2,1,0:T(8,128)S(1)} %get-tuple-element.89), channel_id=1, source_target_pairs={{0,1},{1,2},{2,3},{3,4},{4,5},{5,6},{6,7},{7,8},{8,9},{9,10},{10,1... | collective-permute-start | bytes 6291464 | tf_op jit(solution)/shard_map/ppermute | solution.py:17
  128.7 82.1 %collective-permute-done.4 = f32[2,128,2048]{2,1,0:T(8,128)S(1)} collective-permute-done((f32[2,128,2048]{2,1,0:T(8,128)S(1)}, f32[2,128,2048]{2,1,0:T(8,128)S(1)}, u32[]{:S(2)}, u32[]{:S(2)}) %collective-permute-start.4) | collective-permute-done | bytes 2097184 | tf_op jit(solution)/shard_map/ppermute | solution.py:17
  210.8 1.9 collective-permute-done.3
  212.7 1.4 fusion.9
  214.1 1.3 collective-permute-start.5
  215.4 1.2 copy.42
  216.7 2.4 fusion.15
  219.1 0.2 copy.41
  219.3 27.5 %collective-permute-done.5 = bf16[2,128,2048]{2,1,0:T(8,128)(2,1)S(1)} collective-permute-done((bf16[2,128,2048]{2,1,0:T(8,128)(2,1)}, bf16[2,128,2048]{2,1,0:T(8,128)(2,1)S(1)}, u32[]{:S(2)}, u32[]{:S(2)}) %collective-permute-start.5) | collective-permute-done | bytes 1048608 | tf_op jit(solution)/shard_map/ppermute | solution.py:17
  246.9 1.1 fusion.18
  (9 shorter events, 0.0 us)
Async XLA Ops:
  0.6 33.1 %copy-start.5 = (bf16[1,1,128,2048]{3,2,1,0:T(8,128)(2,1)S(1)}, bf16[1,1,128,2048]{3,2,1,0:T(8,128)(2,1)}, u32[]{:S(2)}) copy-start(bf16[1,1,128,2048]{3,2,1,0:T(8,128)(2,1)} %param.14) | copy-start | bytes 1572868
  0.6 33.4 %copy-start.7 = (s32[1,1,2]{2,1,0:T(1,128)S(1)}, s32[1,1,2]{2,1,0:T(1,128)}, u32[]{:S(2)}) copy-start(s32[1,1,2]{2,1,0:T(1,128)} %param.16) | copy-start | bytes 28
  0.7 41.0 %copy-start.8 = (s32[1,128]{1,0:T(1,128)S(1)}, s32[1,128]{1,0:T(1,128)}, u32[]{:S(2)}) copy-start(s32[1,128]{1,0:T(1,128)} %param.17) | copy-start | bytes 1540
  2.0 25.9 %collective-permute-start = (bf16[2,128,2048]{2,1,0:T(8,128)(2,1)S(1)}, bf16[2,128,2048]{2,1,0:T(8,128)(2,1)S(1)}, u32[]{:S(2)}, u32[]{:S(2)}) collective-permute-start(bf16[2,128,2048]{2,1,0:T(8,128)(2,1)S(1)} %pad_maximum_fusion.1), channel_id=1, source_target_pairs={{0,256},{1,257},{2,258},{3,259},{4,260},{5,261},{6,262},{7,263},{8... | collective-permute-start | bytes 3145736 | tf_op jit(solution)/shard_map/ppermute | solution.py:17
  27.9 29.3 %collective-permute-start.1 = (bf16[2,128,2048]{2,1,0:T(8,128)(2,1)S(1)}, bf16[2,128,2048]{2,1,0:T(8,128)(2,1)}, u32[]{:S(2)}, u32[]{:S(2)}) collective-permute-start(bf16[2,128,2048]{2,1,0:T(8,128)(2,1)S(1)} %collective-permute-done), channel_id=1, source_target_pairs={{0,1},{1,2},{2,3},{3,4},{4,5},{5,6},{6,7},{7,8},{8,9},{9,10},{10,1... | collective-permute-start | bytes 3145736 | tf_op jit(solution)/shard_map/ppermute | solution.py:27
  34.0 36.0 %collective-permute-start.2 = (bf16[2,128,2048]{2,1,0:T(8,128)(2,1)S(1)}, bf16[2,128,2048]{2,1,0:T(8,128)(2,1)}, u32[]{:S(2)}, u32[]{:S(2)}) collective-permute-start(bf16[2,128,2048]{2,1,0:T(8,128)(2,1)S(1)} %collective-permute-done), channel_id=1, source_target_pairs={{1,0},{2,1},{3,2},{4,3},{5,4},{6,5},{7,6},{8,7},{9,8},{10,9},{11,1... | collective-permute-start | bytes 3145736 | tf_op jit(solution)/shard_map/ppermute | solution.py:28
  72.9 1.6 copy-start.6
  83.1 2.1 copy-start.4
  86.1 1.7 copy-start.2
  96.1 1.2 copy-start.3
  97.4 2.8 %copy-start.1 = (f32[384,2048]{1,0:T(8,128)}, f32[384,2048]{1,0:T(8,128)S(1)}, u32[]{:S(2)}) copy-start(f32[384,2048]{1,0:T(8,128)S(1)} %constant_dynamic-update-slice_fusion.3) | copy-start | bytes 9437188
  102.7 2.5 %copy-start = (f32[1,384,2048]{2,1,0:T(8,128)S(1)}, f32[1,384,2048]{2,1,0:T(8,128)}, u32[]{:S(2)}) copy-start(f32[1,384,2048]{2,1,0:T(8,128)} %copy.60) | copy-start | bytes 9437188
  107.4 103.4 %collective-permute-start.4 = (f32[2,128,2048]{2,1,0:T(8,128)S(1)}, f32[2,128,2048]{2,1,0:T(8,128)S(1)}, u32[]{:S(2)}, u32[]{:S(2)}) collective-permute-start(f32[2,128,2048]{2,1,0:T(8,128)S(1)} %get-tuple-element.90), channel_id=1, source_target_pairs={{1,0},{2,1},{3,2},{4,3},{5,4},{6,5},{7,6},{8,7},{9,8},{10,9},{11,1... | collective-permute-start | bytes 6291464 | tf_op jit(solution)/shard_map/ppermute | solution.py:17
  122.7 90.1 %collective-permute-start.3 = (f32[2,128,2048]{2,1,0:T(8,128)S(1)}, f32[2,128,2048]{2,1,0:T(8,128)S(1)}, u32[]{:S(2)}, u32[]{:S(2)}) collective-permute-start(f32[2,128,2048]{2,1,0:T(8,128)S(1)} %get-tuple-element.89), channel_id=1, source_target_pairs={{0,1},{1,2},{2,3},{3,4},{4,5},{5,6},{6,7},{7,8},{8,9},{9,10},{10,1... | collective-permute-start | bytes 6291464 | tf_op jit(solution)/shard_map/ppermute | solution.py:17
  214.1 32.7 %collective-permute-start.5 = (bf16[2,128,2048]{2,1,0:T(8,128)(2,1)}, bf16[2,128,2048]{2,1,0:T(8,128)(2,1)S(1)}, u32[]{:S(2)}, u32[]{:S(2)}) collective-permute-start(bf16[2,128,2048]{2,1,0:T(8,128)(2,1)} %fusion.9), channel_id=1, source_target_pairs={{256,0},{257,1},{258,2},{259,3},{260,4},{261,5},{262,6},{263,7},{2... | collective-permute-start | bytes 3145736 | tf_op jit(solution)/shard_map/ppermute | solution.py:17
where the time goes:
time: 249 us; the launch traced here: 248 us
  waiting for transfers between devices  161 us (65%)
  starting transfers between devices  34.9 us (14%)
  local copies, waits for them, and re-layouts  28.8 us (12%)
  other arithmetic  10.1 us (4%)
  matrix products  9.64 us (4%)
  between operations  3.58 us (1%)
    ppermute x4, waiting for transfers between devices, shifted(): return lax.ppermute(array, axis, pairs)  134 us
    ppermute x4, starting transfers between devices, shifted(): return lax.ppermute(array, axis, pairs)  26.1 us
    ppermute x1, waiting for transfers between devices, padded(): before = lax.ppermute(last, axis, up)  15.5 us
    ppermute x1, waiting for transfers between devices, padded(): after = lax.ppermute(first, axis, down)  11.4 us
    unnamed x24, local copies, waits for them, and re-layouts  9 us
    slice x3, local copies, waits for them, and re-layouts, step(): dvalue[slot * BLK:(slot + 1) * BLK]  8.29 us
  transfers between devices with their start and end apart: 6, of which 6 were waited for; matrix products, arithmetic and copies ran while one was open for 3% of the time, Pallas kernels for 0%

commit v1 on v0

v1 whole, which is shorter than its diff:
```python
import functools

import jax
import jax.numpy as jnp
from jax import lax
from jax.experimental import pallas as pl
from jax.experimental.pallas import tpu as pltpu
from jax.sharding import PartitionSpec as P

HDIM = 64
BLK = 128
CW = 256
LANES = 128
SCALE = HDIM**-0.5
LOG2E = 1.4426950408889634
BIG = 1e30
MESH = pl.DeviceIdType.MESH
NT = (((1,), (1,)), ((), ()))
NN = (((1,), (0,)), ((), ()))


def dot(a, b, dims):
    return lax.dot_general(a, b, dims, preferred_element_type=jnp.float32)


def kernel(
    count,
    align,
    source_len,
    target_len,
    mask,
    first,
    second,
    grad_first,
    grad_second,
    own,
    recv,
    outs,
    keep_rows,
    stat_out,
    stat_in,
    own_sem,
    send_sem,
    recv_sem,
    relay_send,
    relay_recv,
    stat_send,
    stat_recv,
    out_sem,
):
    width = first.shape[-1]
    chunks = width // CW
    heads = CW // HDIM
    section = lax.axis_index("section")
    seq = lax.axis_index("seq")
    step = 2 * section - 1
    ahead = lax.rem(seq + step + count, count)
    behind = lax.rem(seq - step + count, count)
    partner = {"section": 1 - section, "seq": seq}
    side = {"section": 1 - section, "seq": ahead}
    far = {"section": 1 - section, "seq": behind}
    relay_to = {"section": section, "seq": ahead}
    relay_from = {"section": section, "seq": behind}

    inputs = (first, second)
    results = (grad_first, grad_second)

    def columns(c):
        return pl.ds(pl.multiple_of(c * CW, CW), CW)

    def own_copy(arr):
        return pltpu.make_async_copy(inputs[arr].at[0, 0], own.at[arr], own_sem.at[arr])

    def block_copy(slot, arr, c):
        return pltpu.make_async_remote_copy(
            src_ref=inputs[arr].at[0, 0, :, columns(c)],
            dst_ref=recv.at[slot, arr, :, columns(c)],
            send_sem=send_sem.at[slot, arr, c],
            recv_sem=recv_sem.at[slot, arr, c],
            device_id=(partner, side)[slot],
            device_id_type=MESH,
        )

    def relay_copy(c):
        return pltpu.make_async_remote_copy(
            src_ref=recv.at[0, :, :, columns(c)],
            dst_ref=recv.at[2, :, :, columns(c)],
            send_sem=relay_send.at[c],
            recv_sem=relay_recv.at[c],
            device_id=relay_to,
            device_id_type=MESH,
        )

    def stat_copy(slot, c):
        return pltpu.make_async_remote_copy(
            src_ref=stat_out.at[slot, c],
            dst_ref=stat_in.at[slot, c],
            send_sem=stat_send.at[slot, c],
            recv_sem=stat_recv.at[slot, c],
            device_id=(partner, side, far)[slot],
            device_id_type=MESH,
        )

    def out_copy(arr, c):
        return pltpu.make_async_copy(
            outs.at[arr, :, columns(c)],
            results[arr].at[0, 0, :, columns(c)],
            out_sem.at[arr, c],
        )

    for arr in range(2):
        own_copy(arr).start()

    barrier = pltpu.get_barrier_semaphore()
    for peer in (partner, side, far, relay_to, relay_from):
        pl.semaphore_signal(barrier, inc=1, device_id=peer, device_id_type=MESH)
    pl.semaphore_wait(barrier, 5)

    def send_own(c, carry):
        for slot in range(2):
            for arr in range(2):
                block_copy(slot, arr, c).start()
        return carry

    lax.fori_loop(0, chunks, send_own, 0)

    def relay(c):
        for arr in range(2):
            block_copy(0, arr, c).wait_recv()
        relay_copy(c).start()

    for arr in range(2):
        own_copy(arr).wait()

    lane = lax.broadcasted_iota(jnp.int32, (1, LANES), 1)
    row = lax.broadcasted_iota(jnp.int32, (BLK, LANES), 0)
    low_half = lane < HDIM
    half_mask = (
        low_half.astype(jnp.float32).astype(jnp.bfloat16),
        (1.0 - low_half.astype(jnp.float32)).astype(jnp.bfloat16),
    )
    limit = target_len[0]
    source_end = source_len[0]

    @pl.when(section == 1)
    def _():
        missing = 2 * seq - align[0, 0, 0] - align[0, 0, 1]
        lower_missing = missing == -1
        upper_missing = missing == 1
        first_block = jnp.where(lower_missing, seq, seq - 1)
        second_block = jnp.where(upper_missing, seq, seq + 1)
        key_pos = jnp.concatenate([first_block * BLK + lane, second_block * BLK + lane], axis=1)
        key_valid = key_pos < source_end
        live_lane = (seq * BLK + lane < limit).astype(jnp.float32)
        keep_lane = live_lane * (mask[...] == 1).astype(jnp.float32)
        keep_rows[...] = jnp.broadcast_to(keep_lane, (BLK, LANES)).T
        listed = tuple(
            jnp.where(missing == offset, jnp.float32(0.0), jnp.float32(1.0)) for offset in (0, 1, -1)
        )
        stat_lane = lax.broadcasted_iota(jnp.int32, (BLK, LANES), 1)
        stat_row = lax.broadcasted_iota(jnp.int32, (2 * heads, LANES), 0)

        relay(0)
        relay(1)

        def body(c, carry):
            for arr in range(2):
                block_copy(1, arr, c).wait_recv()
            relay_copy(c).wait_recv()
            live = seq * BLK + row < limit
            stats = jnp.zeros((BLK, LANES), jnp.float32)
            saved = []
            for pair in range(CW // LANES):
                cols = pl.ds(pl.multiple_of(c * CW + pair * LANES, LANES), LANES)
                query = own[0, :, cols]
                cot = own[1, :, cols]
                kv = []
                for arr in range(2):
                    middle = recv[0, arr, :, cols]
                    lower = lax.select(lower_missing, middle, recv[2, arr, :, cols])
                    upper = lax.select(upper_missing, middle, recv[1, arr, :, cols])
                    kv.append(jnp.concatenate([lower, upper], axis=0))
                keys, values = kv
                halves = []
                for half in range(2):
                    head = 2 * pair + half
                    cot_half = cot * half_mask[half]
                    scores = dot(query * half_mask[half], keys, NT) * (SCALE * LOG2E)
                    scores = jnp.where(key_valid, scores, -BIG)
                    peak = jnp.max(scores, axis=-1, keepdims=True)
                    expo = jnp.exp2(scores - peak)
                    total = jnp.sum(expo, axis=-1, keepdims=True)
                    probs = expo * (1.0 / total)
                    attended = dot(probs.astype(jnp.bfloat16), values, NN)
                    out_low = jnp.where(live, attended, 0.0).astype(jnp.bfloat16).astype(jnp.float32)
                    delta = jnp.sum(cot_half.astype(jnp.float32) * out_low, axis=-1, keepdims=True)
                    lse = peak + jnp.log(total) * LOG2E
                    stats = jnp.where(stat_lane == head, lse, stats)
                    stats = jnp.where(stat_lane == heads + head, delta, stats)
                    halves.append(out_low)
                    saved.append((cot_half, keys, values, probs, delta))
                outs[1, :, cols] = jnp.where(low_half, halves[0], halves[1]).astype(jnp.bfloat16)
            stats = stats.T[: 2 * heads]
            for slot in range(3):
                kept = keep_lane * listed[slot]
                stat_out[slot, c] = jnp.where((stat_row >= heads) | (kept == 1.0), stats, BIG)
            for slot in range(3):
                stat_copy(slot, c).start()

            @pl.when(c + 2 < chunks)
            def _():
                relay(c + 2)

            out_copy(1, c).start()
            for pair in range(CW // LANES):
                cols = pl.ds(pl.multiple_of(c * CW + pair * LANES, LANES), LANES)
                halves = []
                for half in range(2):
                    cot_half, keys, values, probs, delta = saved[2 * pair + half]
                    dprob = dot(cot_half, values, NT)
                    dscore = (probs * (dprob - delta)).astype(jnp.bfloat16)
                    halves.append(dot(dscore, keys, NN))
                dquery = jnp.where(low_half, halves[0], halves[1]) * SCALE
                dquery = jnp.where(keep_rows[...] == 1.0, dquery, 0.0)
                outs[0, :, cols] = dquery.astype(jnp.bfloat16)
            out_copy(0, c).start()
            return carry

        lax.fori_loop(0, chunks, body, 0)

        def drain(c, carry):
            for slot in range(3):
                stat_copy(slot, c).wait_send()
            return carry

        lax.fori_loop(0, chunks, drain, 0)

    @pl.when(section == 0)
    def _():
        def relay_all(c, carry):
            relay(c)
            return carry

        lax.fori_loop(0, chunks, relay_all, 0)

        def body(c, carry):
            for arr in range(2):
                block_copy(1, arr, c).wait_recv()
            relay_copy(c).wait_recv()
            for slot in range(3):
                stat_copy(slot, c).wait_recv()
            valid = seq * BLK + row < source_end
            stats = jnp.concatenate([stat_in[slot, c] for slot in range(3)], axis=1)
            for pair in range(CW // LANES):
                cols = pl.ds(pl.multiple_of(c * CW + pair * LANES, LANES), LANES)
                keys = own[0, :, cols]
                values = own[1, :, cols]
                queries = recv[:, 0, :, cols].reshape(3 * BLK, LANES)
                cots = recv[:, 1, :, cols].reshape(3 * BLK, LANES)
                key_halves = []
                value_halves = []
                for half in range(2):
                    head = 2 * pair + half
                    scores = dot(keys * half_mask[half], queries, NT) * (SCALE * LOG2E)
                    probs = jnp.exp2(scores - stats[head : head + 1])
                    dprob = dot(values * half_mask[half], cots, NT)
                    dscore = probs * (dprob - stats[heads + head : heads + head + 1])
                    value_halves.append(dot(probs.astype(jnp.bfloat16), cots, NN))
                    key_halves.append(dot(dscore.astype(jnp.bfloat16), queries, NN))
                dkey = jnp.where(low_half, key_halves[0], key_halves[1]) * SCALE
                dvalue = jnp.where(low_half, value_halves[0], value_halves[1])
                outs[0, :, cols] = jnp.where(valid, dkey, 0.0).astype(jnp.bfloat16)
                outs[1, :, cols] = jnp.where(valid, dvalue, 0.0).astype(jnp.bfloat16)
            for arr in range(2):
                out_copy(arr, c).start()
            return carry

        lax.fori_loop(0, chunks, body, 0)

    def drain(c, carry):
        for slot in range(2):
            for arr in range(2):
                block_copy(slot, arr, c).wait_send()
        relay_copy(c).wait_send()
        for arr in range(2):
            out_copy(arr, c).wait()
        return carry

    lax.fori_loop(0, chunks, drain, 0)


def on_device(first_rows, second_rows, alignment, diffusion_mask, source_length, target_length):
    count = lax.axis_size("seq")
    width = first_rows.shape[3]
    chunks = width // CW
    heads = CW // HDIM
    shape = jax.ShapeDtypeStruct(first_rows.shape, jnp.bfloat16)
    anywhere = pl.BlockSpec(memory_space=pl.ANY)
    scalars = pl.BlockSpec(memory_space=pltpu.SMEM)
    return pl.pallas_call(
        functools.partial(kernel, count),
        out_shape=(shape, shape),
        in_specs=[
            scalars,
            scalars,
            scalars,
            pl.BlockSpec(memory_space=pltpu.VMEM),
            anywhere,
            anywhere,
        ],
        out_specs=(anywhere, anywhere),
        scratch_shapes=[
            pltpu.VMEM((2, BLK, width), jnp.bfloat16),
            pltpu.VMEM((3, 2, BLK, width), jnp.bfloat16),
            pltpu.VMEM((2, BLK, width), jnp.bfloat16),
            pltpu.VMEM((BLK, LANES), jnp.float32),
            pltpu.VMEM((3, chunks, 2 * heads, BLK), jnp.float32),
            pltpu.VMEM((3, chunks, 2 * heads, BLK), jnp.float32),
            pltpu.SemaphoreType.DMA((2,)),
            pltpu.SemaphoreType.DMA((2, 2, chunks)),
            pltpu.SemaphoreType.DMA((2, 2, chunks)),
            pltpu.SemaphoreType.DMA((chunks,)),
            pltpu.SemaphoreType.DMA((chunks,)),
            pltpu.SemaphoreType.DMA((3, chunks)),
            pltpu.SemaphoreType.DMA((3, chunks)),
            pltpu.SemaphoreType.DMA((2, chunks)),
        ],
        compiler_params=pltpu.CompilerParams(collective_id=0, has_side_effects=True),
    )(alignment, source_length, target_length, diffusion_mask, first_rows, second_rows)


def solution(mesh):
    placed = (
        P("section", "sample", "seq", None),
        P("section", "sample", "seq", None),
        P("sample", "seq", None),
        P("sample", "seq"),
        P("sample"),
        P("sample"),
    )
    return jax.shard_map(
        on_device,
        mesh=mesh,
        in_specs=placed,
        out_specs=(P("section", "sample", "seq", None), P("section", "sample", "seq", None)),
        check_vma=False,
    )
```

time: 249 us -> 72.4 us (0.29)
  the two profiles are of different devices: /device:TPU:450 before, /device:TPU:320 now
where the time goes in v1:
time: 72.4 us; the launch traced here: 72.3 us
  Pallas kernels  67.6 us (93%)
  local copies, waits for them, and re-layouts  2.74 us (4%)
  between operations  1.94 us (3%)
    pallas_call x1, Pallas kernels, on_device(): pl.pallas_call(functools.partial(kernel, count), out_shape=(shape, shape)...  67.6 us
    unnamed x4, local copies, waits for them, and re-layouts  2.74 us

profile of v1, /device:TPU:320, one launch (start us, length us, event | category | flops | bytes accessed | tf_op | source)
XLA Modules:
  0.0 72.3 jit_solution(9864784673129828505)
XLA Ops:
  1.9 67.6 %shard_map.77 = (bf16[1,1,128,2048]{3,2,1,0:T(8,128)(2,1)}, bf16[1,1,128,2048]{3,2,1,0:T(8,128)(2,1)}) custom-call(s32[1,1,2]{2,1,0:T(1,128)} %align.1, s32[1]{0:T(128)S(6)} %copy.10.source_len, s32[1]{0:T(128)S(6)} %copy.11.target_len, s32[1,128]{1,0:T(1,128)} %mask.1, bf16[1,1,128,2048]{3,2,1,0:T(8,128)(2,1)} %first.1, bf16[1,1,128,2048]{3,2,1,0:T(8,128)(2,1)} %second.1), custom_call_target="tpu_custom_call" | custom-call | tf_op jit(solution)/shard_map/pallas_call | solution.py:300
  69.5 0.0 copy-start
  69.5 1.9 %copy.12 = bf16[1,1,128,2048]{3,2,1,0:T(8,128)(2,1)} copy(bf16[1,1,128,2048]{3,2,1,0:T(8,128)(2,1)} %get-tuple-element.4) | data formatting | bytes 1048576
  71.5 0.0 copy-done
  71.5 0.8 %copy.13 = bf16[1,1,128,2048]{3,2,1,0:T(8,128)(2,1)} copy(bf16[1,1,128,2048]{3,2,1,0:T(8,128)(2,1)S(1)} %copy-done) | data formatting | bytes 1048576
Async XLA Ops:
  69.5 2.0 %copy-start = (bf16[1,1,128,2048]{3,2,1,0:T(8,128)(2,1)S(1)}, bf16[1,1,128,2048]{3,2,1,0:T(8,128)(2,1)}, u32[]{:S(2)}) copy-start(bf16[1,1,128,2048]{3,2,1,0:T(8,128)(2,1)} %get-tuple-element.5) | copy-start | bytes 1572868

commit v2 on v1

v2 whole, which is shorter than its diff:
```python
import functools

import jax
import jax.numpy as jnp
from jax import lax
from jax.experimental import pallas as pl
from jax.experimental.pallas import tpu as pltpu
from jax.sharding import PartitionSpec as P

HDIM = 64
BLK = 128
CW = 256
OWN = 128
AHEAD = 3
LANES = 128
SCALE = HDIM**-0.5
LOG2E = 1.4426950408889634
BIG = 1e30
MESH = pl.DeviceIdType.MESH
NT = (((1,), (1,)), ((), ()))
NN = (((1,), (0,)), ((), ()))


def dot(a, b, dims):
    return lax.dot_general(a, b, dims, preferred_element_type=jnp.float32)


def kernel(
    count,
    align_in,
    source_len,
    target_len,
    mask_in,
    first,
    second,
    grad_first,
    grad_second,
    align,
    mask,
    own,
    recv,
    keep_rows,
    stat_out,
    stat_in,
    own_sem,
    send_sem,
    recv_sem,
    relay_send,
    relay_recv,
    stat_send,
    stat_recv,
    small_sem,
):
    width = first.shape[-1]
    chunks = width // CW
    heads = CW // HDIM
    section = lax.axis_index("section")
    seq = lax.axis_index("seq")
    step = 2 * section - 1
    ahead = lax.rem(seq + step + count, count)
    behind = lax.rem(seq - step + count, count)
    partner = {"section": 1 - section, "seq": seq}
    side = {"section": 1 - section, "seq": ahead}
    far = {"section": 1 - section, "seq": behind}
    relay_to = {"section": section, "seq": ahead}
    relay_from = {"section": section, "seq": behind}

    inputs = (first, second)

    def columns(c):
        return pl.ds(pl.multiple_of(c * CW, CW), CW)

    def own_copy(arr):
        return pltpu.make_async_copy(inputs[arr].at[0, 0], own.at[arr], own_sem.at[arr])

    def block_copy(slot, arr, g):
        part = pl.ds(pl.multiple_of(g * OWN, OWN), OWN)
        return pltpu.make_async_remote_copy(
            src_ref=inputs[arr].at[0, 0, :, part],
            dst_ref=recv.at[slot, arr, :, part],
            send_sem=send_sem.at[slot, arr, g],
            recv_sem=recv_sem.at[slot, arr, g],
            device_id=(partner, side)[slot],
            device_id_type=MESH,
        )

    def relay_copy(c):
        return pltpu.make_async_remote_copy(
            src_ref=recv.at[0, :, :, columns(c)],
            dst_ref=recv.at[2, :, :, columns(c)],
            send_sem=relay_send.at[c],
            recv_sem=relay_recv.at[c],
            device_id=relay_to,
            device_id_type=MESH,
        )

    def stat_copy(slot, c):
        return pltpu.make_async_remote_copy(
            src_ref=stat_out.at[slot, c],
            dst_ref=stat_in.at[slot, c],
            send_sem=stat_send.at[slot, c],
            recv_sem=stat_recv.at[slot, c],
            device_id=(partner, side, far)[slot],
            device_id_type=MESH,
        )

    has_ahead = (seq + step >= 0) & (seq + step < count)
    has_behind = (seq - step >= 0) & (seq - step < count)

    barrier = pltpu.get_barrier_semaphore()

    def greet(*peers):
        for peer in peers:
            pl.semaphore_signal(barrier, inc=1, device_id=peer, device_id_type=MESH)

    greet(partner)
    pl.when(has_ahead)(lambda: greet(side, relay_to))
    pl.when(has_behind)(lambda: greet(far, relay_from))

    small = [
        pltpu.make_async_copy(src, dst, small_sem.at[i])
        for i, (src, dst) in enumerate(
            ((align_in, align), (mask_in, mask))
        )
    ]
    for copy in small:
        copy.start()
    for arr in range(2):
        own_copy(arr).start()
    pl.semaphore_wait(barrier, 1 + 2 * has_ahead.astype(jnp.int32) + 2 * has_behind.astype(jnp.int32))

    def for_slots(slots, act):
        conditions = (None, has_ahead, has_behind)
        for slot in slots:
            if slot == 0:
                act(slot)
            else:
                pl.when(conditions[slot])(functools.partial(act, slot))

    def send_own(g, carry):
        def act(slot):
            for arr in range(2):
                block_copy(slot, arr, g).start()

        for_slots((0, 1), act)
        return carry

    lax.fori_loop(0, width // OWN, send_own, 0)

    def relay(c):
        for part in range(CW // OWN):
            for arr in range(2):
                block_copy(0, arr, c * (CW // OWN) + part).wait_recv()
        pl.when(has_ahead)(lambda: relay_copy(c).start())

    groups = width // OWN
    waited = jnp.where(has_behind, groups - 1, groups)

    def wait_ahead(g, carry):
        for arr in range(2):
            block_copy(1, arr, g).wait_recv()
        return carry

    pl.when(has_ahead)(lambda: lax.fori_loop(0, waited, wait_ahead, None))

    def relay_some(c, carry):
        relay(c)
        return carry

    lax.fori_loop(0, jnp.where(section == 1, min(AHEAD, chunks), chunks), relay_some, 0)

    for copy in small:
        copy.wait()
    for arr in range(2):
        own_copy(arr).wait()

    lane = lax.broadcasted_iota(jnp.int32, (1, LANES), 1)
    row = lax.broadcasted_iota(jnp.int32, (BLK, LANES), 0)
    low_half = lane < HDIM
    half_mask = (
        low_half.astype(jnp.float32).astype(jnp.bfloat16),
        (1.0 - low_half.astype(jnp.float32)).astype(jnp.bfloat16),
    )

    def stacked(block):
        return jnp.concatenate([block * half_mask[0], block * half_mask[1]], axis=0)

    limit = target_len[0]
    source_end = source_len[0]

    @pl.when(section == 1)
    def _():
        missing = 2 * seq - align[0, 0, 0] - align[0, 0, 1]
        lower_missing = missing == -1
        upper_missing = missing == 1
        first_block = jnp.where(lower_missing, seq, seq - 1)
        second_block = jnp.where(upper_missing, seq, seq + 1)
        key_pos = lane - source_end
        key_pos = jnp.concatenate([first_block * BLK + key_pos, second_block * BLK + key_pos], axis=1)
        key_valid = key_pos < 0
        live_lane = (seq * BLK + lane < limit).astype(jnp.float32)
        keep_lane = live_lane * (mask[...] == 1).astype(jnp.float32)
        keep_rows[...] = jnp.broadcast_to(keep_lane, (BLK, LANES)).T
        listed = tuple(
            jnp.where(missing == offset, jnp.float32(0.0), jnp.float32(1.0)) for offset in (0, 1, -1)
        )
        stat_lane = lax.broadcasted_iota(jnp.int32, (BLK, LANES), 1)
        stat_row = lax.broadcasted_iota(jnp.int32, (2 * heads, LANES), 0)

        def body(c, carry):
            pl.when((c == chunks - 1) & has_ahead)(lambda: lax.fori_loop(waited, groups, wait_ahead, None))
            pl.when(has_behind)(lambda: relay_copy(c).wait_recv())
            live = seq * BLK + jnp.concatenate([row, row], axis=0) < limit
            stats = jnp.zeros((BLK, LANES), jnp.float32)
            saved = []
            for pair in range(CW // LANES):
                cols = pl.ds(pl.multiple_of(c * CW + pair * LANES, LANES), LANES)
                query = own[0, :, cols]
                cot = own[1, :, cols]
                kv = []
                for arr in range(2):
                    middle = recv[0, arr, :, cols]
                    lower = lax.select(lower_missing, middle, recv[2, arr, :, cols])
                    upper = lax.select(upper_missing, middle, recv[1, arr, :, cols])
                    kv.append(jnp.concatenate([lower, upper], axis=0))
                keys, values = kv
                cots = stacked(cot)
                scores = dot(stacked(query), keys, NT) * (SCALE * LOG2E)
                scores = jnp.where(key_valid, scores, -BIG)
                peak = jnp.max(scores, axis=-1, keepdims=True)
                expo = jnp.exp2(scores - peak)
                total = jnp.sum(expo, axis=-1, keepdims=True)
                probs = expo * (1.0 / total)
                attended = dot(probs.astype(jnp.bfloat16), values, NN)
                out_low = jnp.where(live, attended, 0.0).astype(jnp.bfloat16).astype(jnp.float32)
                delta = jnp.sum(cots.astype(jnp.float32) * out_low, axis=-1, keepdims=True)
                lse = peak + jnp.log(total) * LOG2E
                for half in range(2):
                    head = 2 * pair + half
                    rows = slice(half * BLK, (half + 1) * BLK)
                    stats = jnp.where(stat_lane == head, lse[rows], stats)
                    stats = jnp.where(stat_lane == heads + head, delta[rows], stats)
                saved.append((cots, keys, values, probs, delta))
                halves = out_low[:BLK], out_low[BLK:]
                grad_second[0, 0, :, cols] = jnp.where(low_half, halves[0], halves[1]).astype(jnp.bfloat16)
            stats = stats.T[: 2 * heads]
            for slot in range(3):
                kept = keep_lane * listed[slot]
                stat_out[slot, c] = jnp.where((stat_row >= heads) | (kept == 1.0), stats, BIG)
            for_slots((2, 1, 0), lambda slot: stat_copy(slot, c).start())
            pl.when(c + AHEAD < chunks)(lambda: relay(c + AHEAD))

            for pair in range(CW // LANES):
                cols = pl.ds(pl.multiple_of(c * CW + pair * LANES, LANES), LANES)
                cots, keys, values, probs, delta = saved[pair]
                dprob = dot(cots, values, NT)
                dscore = (probs * (dprob - delta)).astype(jnp.bfloat16)
                queries_grad = dot(dscore, keys, NN)
                halves = queries_grad[:BLK], queries_grad[BLK:]
                dquery = jnp.where(low_half, halves[0], halves[1]) * SCALE
                dquery = jnp.where(keep_rows[...] == 1.0, dquery, 0.0)
                grad_first[0, 0, :, cols] = dquery.astype(jnp.bfloat16)
            return carry

        lax.fori_loop(0, chunks, body, 0)

        def drain(c, carry):
            for_slots(range(3), lambda slot: stat_copy(slot, c).wait_send())
            return carry

        lax.fori_loop(0, chunks, drain, 0)

    @pl.when(section == 0)
    def _():
        def absent(slot):
            recv[slot] = jnp.zeros_like(recv[slot])
            stat_in[slot] = jnp.full_like(stat_in[slot], BIG)

        pl.when(jnp.logical_not(has_ahead))(lambda: absent(1))
        pl.when(jnp.logical_not(has_behind))(lambda: absent(2))

        def body(c, carry):
            pl.when((c == chunks - 1) & has_ahead)(lambda: lax.fori_loop(waited, groups, wait_ahead, None))
            pl.when(has_behind)(lambda: relay_copy(c).wait_recv())
            for_slots(range(3), lambda slot: stat_copy(slot, c).wait_recv())
            valid = seq * BLK + row < source_end
            stats = jnp.concatenate([stat_in[slot, c] for slot in range(3)], axis=1)
            for pair in range(CW // LANES):
                cols = pl.ds(pl.multiple_of(c * CW + pair * LANES, LANES), LANES)
                queries = recv[:, 0, :, cols].reshape(3 * BLK, LANES)
                cots = recv[:, 1, :, cols].reshape(3 * BLK, LANES)

                def per_key(base):
                    rows = [stats[base + 2 * pair + half : base + 2 * pair + half + 1] for half in range(2)]
                    return jnp.concatenate([jnp.broadcast_to(line, (BLK, 3 * BLK)) for line in rows], axis=0)

                scores = dot(stacked(own[0, :, cols]), queries, NT) * (SCALE * LOG2E)
                probs = jnp.exp2(scores - per_key(0))
                dprob = dot(stacked(own[1, :, cols]), cots, NT)
                dscore = probs * (dprob - per_key(heads))
                dvalue = dot(probs.astype(jnp.bfloat16), cots, NN)
                dkey = dot(dscore.astype(jnp.bfloat16), queries, NN)
                dkey = jnp.where(low_half, dkey[:BLK], dkey[BLK:]) * SCALE
                dvalue = jnp.where(low_half, dvalue[:BLK], dvalue[BLK:])
                grad_first[0, 0, :, cols] = jnp.where(valid, dkey, 0.0).astype(jnp.bfloat16)
                grad_second[0, 0, :, cols] = jnp.where(valid, dvalue, 0.0).astype(jnp.bfloat16)
            return carry

        lax.fori_loop(0, chunks, body, 0)

    def drain_own(g, carry):
        def act(slot):
            for arr in range(2):
                block_copy(slot, arr, g).wait_send()

        for_slots((0, 1), act)
        return carry

    def drain_relay(c, carry):
        relay_copy(c).wait_send()
        return carry

    lax.fori_loop(0, groups, drain_own, 0)
    pl.when(has_ahead)(lambda: lax.fori_loop(0, chunks, drain_relay, None))


def store(first, second, grad_first, grad_second, sems):
    copies = (
        pltpu.make_async_copy(first, grad_first, sems.at[0]),
        pltpu.make_async_copy(second, grad_second, sems.at[1]),
    )
    for copy in copies:
        copy.start()
    for copy in copies:
        copy.wait()


def on_device(first_rows, second_rows, alignment, diffusion_mask, source_length, target_length):
    count = lax.axis_size("seq")
    width = first_rows.shape[3]
    chunks = width // CW
    heads = CW // HDIM
    shape = jax.ShapeDtypeStruct(first_rows.shape, jnp.bfloat16)
    anywhere = pl.BlockSpec(memory_space=pl.ANY)
    on_chip = pl.BlockSpec(memory_space=pltpu.VMEM)
    in_hbm = pl.BlockSpec(memory_space=pltpu.HBM)
    scalars = pl.BlockSpec(memory_space=pltpu.SMEM)

    def kept(array):
        return pltpu.with_memory_space_constraint(array, pltpu.HBM)

    made = pl.pallas_call(
        functools.partial(kernel, count),
        out_shape=(shape, shape),
        in_specs=[in_hbm, scalars, scalars, in_hbm, in_hbm, in_hbm],
        out_specs=(on_chip, on_chip),
        scratch_shapes=[
            pltpu.SMEM(alignment.shape, jnp.int32),
            pltpu.VMEM(diffusion_mask.shape, jnp.int32),
            pltpu.VMEM((2, BLK, width), jnp.bfloat16),
            pltpu.VMEM((3, 2, BLK, width), jnp.bfloat16),
            pltpu.VMEM((BLK, LANES), jnp.float32),
            pltpu.VMEM((3, chunks, 2 * heads, BLK), jnp.float32),
            pltpu.VMEM((3, chunks, 2 * heads, BLK), jnp.float32),
            pltpu.SemaphoreType.DMA((2,)),
            pltpu.SemaphoreType.DMA((2, 2, width // OWN)),
            pltpu.SemaphoreType.DMA((2, 2, width // OWN)),
            pltpu.SemaphoreType.DMA((chunks,)),
            pltpu.SemaphoreType.DMA((chunks,)),
            pltpu.SemaphoreType.DMA((3, chunks)),
            pltpu.SemaphoreType.DMA((3, chunks)),
            pltpu.SemaphoreType.DMA((2,)),
        ],
        compiler_params=pltpu.CompilerParams(
            collective_id=0, has_side_effects=True, vmem_limit_bytes=24 << 20
        ),
    )(
        kept(alignment),
        source_length,
        target_length,
        kept(diffusion_mask),
        kept(first_rows),
        kept(second_rows),
    )
    return pl.pallas_call(
        store,
        out_shape=(shape, shape),
        in_specs=[on_chip, on_chip],
        out_specs=(anywhere, anywhere),
        scratch_shapes=[pltpu.SemaphoreType.DMA((2,))],
        compiler_params=pltpu.CompilerParams(vmem_limit_bytes=4 << 20),
    )(*made)


def solution(mesh):
    placed = (
        P("section", "sample", "seq", None),
        P("section", "sample", "seq", None),
        P("sample", "seq", None),
        P("sample", "seq"),
        P("sample"),
        P("sample"),
    )
    return jax.shard_map(
        on_device,
        mesh=mesh,
        in_specs=placed,
        out_specs=(P("section", "sample", "seq", None), P("section", "sample", "seq", None)),
        check_vma=False,
    )
```

time: 72.4 us -> 64.7 us (0.89)
  the two profiles are of different devices: /device:TPU:320 before, /device:TPU:134 now
where the time goes in v2:
time: 64.7 us; the launch traced here: 64.6 us
  Pallas kernels  62.7 us (97%)
  between operations  1.93 us (3%)
    pallas_call x1, Pallas kernels, on_device(): pl.pallas_call(functools.partial(kernel, count), out_shape=(shape, shape)...  61.7 us

profile of v2, /device:TPU:134, one launch (start us, length us, event | category | flops | bytes accessed | tf_op | source)
XLA Modules:
  0.0 64.6 jit_solution(10808464460449912599)
XLA Ops:
  1.9 61.7 %shard_map.77 = (bf16[1,1,128,2048]{3,2,1,0:T(8,128)(2,1)S(1)}, bf16[1,1,128,2048]{3,2,1,0:T(8,128)(2,1)S(1)}) custom-call(s32[1,1,2]{2,1,0:T(1,128)} %align_in.1, s32[1]{0:T(128)S(6)} %copy.8.source_len, s32[1]{0:T(128)S(6)} %copy.9.target_len, s32[1,128]{1,0:T(1,128)} %mask_in.1, bf16[1,1,128,2048]{3,2,1,0:T(8,128)(2,1)} %first.1, ...), custom_call_target="tpu_custom_call" | custom-call | tf_op jit(solution)/shard_map/pallas_call | solution.py:352
  63.6 1.0 %shard_map.78 = (bf16[1,1,128,2048]{3,2,1,0:T(8,128)(2,1)}, bf16[1,1,128,2048]{3,2,1,0:T(8,128)(2,1)}) custom-call(bf16[1,1,128,2048]{3,2,1,0:T(8,128)(2,1)S(1)} %get-tuple-element.4.first, bf16[1,1,128,2048]{3,2,1,0:T(8,128)(2,1)S(1)} %get-tuple-element.5.second), custom_call_target="tpu_custom_call" | custom-call | tf_op jit(solution)/shard_map/pallas_call | solution.py:385

commit v3 on v2

--- a/solution.py
+++ b/solution.py
@@ -11,7 +11,7 @@
 BLK = 128
 CW = 256
 OWN = 128
-AHEAD = 3
+AHEAD = 4
 LANES = 128
 SCALE = HDIM**-0.5
 LOG2E = 1.4426950408889634
@@ -114,8 +114,7 @@
             pl.semaphore_signal(barrier, inc=1, device_id=peer, device_id_type=MESH)
 
     greet(partner)
-    pl.when(has_ahead)(lambda: greet(side, relay_to))
-    pl.when(has_behind)(lambda: greet(far, relay_from))
+    pl.when(has_ahead)(lambda: greet(side))
 
     small = [
         pltpu.make_async_copy(src, dst, small_sem.at[i])
@@ -127,7 +126,7 @@
         copy.start()
     for arr in range(2):
         own_copy(arr).start()
-    pl.semaphore_wait(barrier, 1 + 2 * has_ahead.astype(jnp.int32) + 2 * has_behind.astype(jnp.int32))
+    pl.semaphore_wait(barrier, 1 + has_ahead.astype(jnp.int32))
 
     def for_slots(slots, act):
         conditions = (None, has_ahead, has_behind)
@@ -154,7 +153,7 @@
         pl.when(has_ahead)(lambda: relay_copy(c).start())
 
     groups = width // OWN
-    waited = jnp.where(has_behind, groups - 1, groups)
+    waited = jnp.where(has_behind, groups - 2, groups)
 
     def wait_ahead(g, carry):
         for arr in range(2):

time: 64.7 us -> 64 us (0.989)
  the two profiles are of different devices: /device:TPU:134 before, /device:TPU:320 now
where the time goes in v3:
time: 64 us; the launch traced here: 63.4 us
  Pallas kernels  61.5 us (96%)
  between operations  1.93 us (3%)
    pallas_call x1, Pallas kernels, on_device(): pl.pallas_call(functools.partial(kernel, count), out_shape=(shape, shape)...  60.5 us

profile of v3, /device:TPU:320, one launch (start us, length us, event | category | flops | bytes accessed | tf_op | source)
XLA Modules:
  0.0 63.4 jit_solution(12765407096683181074)
XLA Ops:
  1.9 60.5 %shard_map.77 = (bf16[1,1,128,2048]{3,2,1,0:T(8,128)(2,1)S(1)}, bf16[1,1,128,2048]{3,2,1,0:T(8,128)(2,1)S(1)}) custom-call(s32[1,1,2]{2,1,0:T(1,128)} %align_in.1, s32[1]{0:T(128)S(6)} %copy.8.source_len, s32[1]{0:T(128)S(6)} %copy.9.target_len, s32[1,128]{1,0:T(1,128)} %mask_in.1, bf16[1,1,128,2048]{3,2,1,0:T(8,128)(2,1)} %first.1, ...), custom_call_target="tpu_custom_call" | custom-call | tf_op jit(solution)/shard_map/pallas_call | solution.py:351
  62.4 1.0 %shard_map.78 = (bf16[1,1,128,2048]{3,2,1,0:T(8,128)(2,1)}, bf16[1,1,128,2048]{3,2,1,0:T(8,128)(2,1)}) custom-call(bf16[1,1,128,2048]{3,2,1,0:T(8,128)(2,1)S(1)} %get-tuple-element.4.first, bf16[1,1,128,2048]{3,2,1,0:T(8,128)(2,1)S(1)} %get-tuple-element.5.second), custom_call_target="tpu_custom_call" | custom-call | tf_op jit(solution)/shard_map/pallas_call | solution.py:384
